TPU v7x, 32 devices: a whole 2x2x4 slice. The times are simulated.
32 devices in a mesh: sector: 8 (over z, y), mpo: 4 (over x, core).
Axes of the slice: x: 2, y: 2, z: 4, core: 2. Of those that a mesh axis runs over, the one named last changes fastest.
Arguments:
- vectors: bfloat16 [16, 8, 256, 256], P(None, 'sector'), may hold values from -6 to 6
- left_env: bfloat16 [16, 8, 256, 256], P('mpo', 'sector'), may hold values from -4 to 4
- right_env: bfloat16 [16, 8, 256, 256], P('mpo', 'sector'), may hold values from -4 to 4
- bond_shift: int32 [16], replicated, may hold values from -1 to 1, as said below
Outputs:
- sigma: bfloat16 [16, 8, 256, 256], P('mpo', 'sector')
- intersection: float32 [16, 16], replicated
- ham_small: float32 [16, 16], replicated
Inputs may be any that keep to these rules, and one draw needn't show every extreme that they name: `bond_shift`: every one of -1, 0 and 1 occurs.
All inputs are finite; a program needn't handle non-finite values.
Results may differ from a plain program's by a relative error of at most 0.0034.
Values may be sent and summed in bfloat16 or wider, within the bound.
A program may use at most 128 MiB of HBM per device.

v0:
```python
import jax
import jax.numpy as jnp
from jax import lax
from jax.sharding import PartitionSpec as P


def with_halo(cells, sides, width):
    for axis, dim in sides:
        count = lax.axis_size(axis)
        ends = count - 1
        head = lax.slice_in_dim(cells, 0, width, axis=dim)
        tail = lax.slice_in_dim(cells, cells.shape[dim] - width, cells.shape[dim], axis=dim)
        cells = jnp.concatenate(
            [
                lax.ppermute(tail, axis, [(i, (i + 1) % count) for i in range(ends)]),
                cells,
                lax.ppermute(head, axis, [((i + 1) % count, i) for i in range(ends)]),
            ],
            axis=dim,
        )
    return cells


def bond_term(extended, lenv, renv, shift):
    source = lax.dynamic_slice_in_dim(extended, 1 + shift, lenv.shape[0], 1)
    left = jnp.einsum("sab,vsbc->vsac", lenv, source, preferred_element_type=jnp.float32).astype(
        jnp.bfloat16
    )
    return jnp.einsum("vsac,scd->vsad", left, renv, preferred_element_type=jnp.float32)


def body(vectors, left_env, right_env, bond_shift):
    group = lax.axis_size("mpo")
    per_owner = vectors.shape[0] // group
    owner_start = lax.axis_index("mpo") * per_owner
    owned = lax.dynamic_slice_in_dim(vectors, owner_start, per_owner, 0)
    extended = with_halo(owned, (("sector", 1),), 1)
    empty = jnp.zeros(owned.shape, jnp.float32)
    lpiece = lax.all_gather(left_env, "mpo", axis=0, tiled=True)
    rpiece = lax.all_gather(right_env, "mpo", axis=0, tiled=True)

    def step(index, accum):
        shift = lax.dynamic_index_in_dim(bond_shift, index, 0, keepdims=False)
        return accum + bond_term(extended, lpiece[index], rpiece[index], shift)

    summed = lax.fori_loop(0, lpiece.shape[0], step, empty)
    sigma = summed.astype(jnp.bfloat16)
    scale = 1.0 / (lax.axis_size("sector") * vectors.shape[1] * vectors.shape[2] * vectors.shape[3])
    zeros_small = jnp.zeros((vectors.shape[0], vectors.shape[0]), jnp.float32)
    ham_cols = jnp.einsum("isab,jsab->ij", vectors, sigma, preferred_element_type=jnp.float32)
    ham_part = lax.dynamic_update_slice(zeros_small, ham_cols, (jnp.int32(0), owner_start))
    full_intersection = jnp.einsum(
        "isab,jsab->ij", vectors, vectors, preferred_element_type=jnp.float32
    )
    intersection = lax.psum(full_intersection, "sector")
    ham_small = lax.psum(ham_part, ("sector", "mpo"))
    return (sigma, intersection * scale, ham_small * scale)


def solution(mesh):
    return jax.shard_map(
        body,
        mesh=mesh,
        in_specs=(
            P(None, "sector", None, None),
            P("mpo", "sector", None, None),
            P("mpo", "sector", None, None),
            P(),
        ),
        out_specs=(P("mpo", "sector", None, None), P(), P()),
        check_vma=False,
    )
```

profile of v0, /device:TPU:0, one launch (start us, length us, event | category | flops | bytes accessed | tf_op | source)
XLA Modules:
  0.0 170.0 jit_solution(12909830077423487255)
XLA Ops:
  7.2 0.7 all-gather.3.cloned.1.call-update
  7.9 0.7 all-gather.5.cloned.1.call-update
  8.7 1.1 constant_dynamic-slice_fusion
  9.9 4.9 %collective-permute-start = (bf16[4,1,256,256]{2,3,0,1:T(8,128)(2,1)S(1)}, bf16[4,1,256,256]{2,3,0,1:T(8,128)(2,1)S(1)}, u32[]{:S(2)}, u32[]{:S(2)}) collective-permute-start(bf16[4,1,256,256]{2,3,0,1:T(8,128)(2,1)S(1)} %copy.29), channel_id=1, source_target_pairs={{0,4},{4,8},{8,12},{12,16},{16,20},{20,24},{24,28},{1,5},{5,9},{9,... | collective-permute-start | bytes 1572872 | tf_op jit(solution)/shard_map/ppermute | solution.py:15
  14.9 1.3 collective-permute-start.1
  16.2 4.9 %fusion.18 = f32[16,16]{1,0:T(8,128)S(1)} fusion(bf16[16,256,256]{2,1,0:T(8,128)(2,1)} %bitcast.55), kind=kOutput, calls=%fused_computation.16 | convolution fusion | flops 33554432 | bytes 2098176 | tf_op jit(solution)/shard_map/isab,jsab->ij/dot_general | solution.py:52
  21.1 29.0 %psum.14 = f32[16,16]{1,0:T(8,128)S(1)} all-reduce(f32[16,16]{1,0:T(8,128)S(1)} %fusion.18), channel_id=1, replica_groups=mesh['sector'=8,'mpo'=4] {'sector'}, use_global_device_ids=true, to_apply=%region_2.3 | all-reduce | flops 256 | bytes 2048 | tf_op jit(solution)/shard_map/psum | solution.py:55
  50.0 0.6 broadcast_multiply_fusion.1
  50.6 0.8 copy-done.1
  51.4 1.4 pad_maximum_fusion
  52.8 6.2 %all-gather.5.cloned.1.call-done = bf16[16,1,256,256]{3,2,1,0:T(8,128)(2,1)} async-done(((bf16[4,1,256,256]{3,2,1,0:T(8,128)(2,1)}), bf16[16,1,256,256]{3,2,1,0:T(8,128)(2,1)}) %all-gather.5.cloned.1.call-update) | async-done | bytes 2097168 | tf_op jit(solution)/shard_map/all_gather | solution.py:39
  59.0 60.5 %while.16 = (s32[]{:T(128)}, f32[4,1,256,256]{2,3,0,1:T(8,128)S(1)}, bf16[16,1,256,256]{3,2,1,0:T(8,128)(2,1)}, s32[16]{0:T(128)S(1)}, bf16[4,3,256,256]{2,3,0,1...) while((s32[]{:T(128)}, ...), condition=%wide.region_1.2_spmd.clone, body=%wide.region_0.1_spmd.clone.sunk | while | flops 269221888 | bytes 2884781 | solution.py:46
  59.0 0.6 dynamic_slice.71
  60.9 1.9 %fusion.32 = f32[4,1,256,256]{2,3,0,1:T(8,128)S(1)} fusion(f32[4,1,256,256]{2,3,0,1:T(8,128)S(1)} %get-tuple-element.245, bf16[4,3,256,256]{2,3,0,1:T(8,128)(2,1)S(1)} %get-tuple-element.258, s32[]{:T(128)S(6)} %select_n.28, pred[]{:T(512)S(6)} %compare.3, bf16[16,1,256,256]{3,2,1,0:T(8,128)(2,1)} %get-tuple-element.259, s32[]{:T(128)} %get-tuple-element.244, ...), kind=kOutput, calls=%fused_computation.1.clone.1 | convolution fusion | flops 269221888 | bytes 2884613 | tf_op jit(solution)/shard_map/while/body/eval_jaxpr/vsac,scd->vsad/dot_general | solution.py:29
  62.8 0.6 dynamic_slice.71
  64.7 1.9 %fusion.32 = f32[4,1,256,256]{2,3,0,1:T(8,128)S(1)} fusion(f32[4,1,256,256]{2,3,0,1:T(8,128)S(1)} %get-tuple-element.245, bf16[4,3,256,256]{2,3,0,1:T(8,128)(2,1)S(1)} %get-tuple-element.258, s32[]{:T(128)S(6)} %select_n.28, pred[]{:T(512)S(6)} %compare.3, bf16[16,1,256,256]{3,2,1,0:T(8,128)(2,1)} %get-tuple-element.259, s32[]{:T(128)} %get-tuple-element.244, ...), kind=kOutput, calls=%fused_computation.1.clone.1 | convolution fusion | flops 269221888 | bytes 2884613 | tf_op jit(solution)/shard_map/while/body/eval_jaxpr/vsac,scd->vsad/dot_general | solution.py:29
  66.6 0.6 dynamic_slice.71
  68.5 1.9 %fusion.32 = f32[4,1,256,256]{2,3,0,1:T(8,128)S(1)} fusion(f32[4,1,256,256]{2,3,0,1:T(8,128)S(1)} %get-tuple-element.245, bf16[4,3,256,256]{2,3,0,1:T(8,128)(2,1)S(1)} %get-tuple-element.258, s32[]{:T(128)S(6)} %select_n.28, pred[]{:T(512)S(6)} %compare.3, bf16[16,1,256,256]{3,2,1,0:T(8,128)(2,1)} %get-tuple-element.259, s32[]{:T(128)} %get-tuple-element.244, ...), kind=kOutput, calls=%fused_computation.1.clone.1 | convolution fusion | flops 269221888 | bytes 2884613 | tf_op jit(solution)/shard_map/while/body/eval_jaxpr/vsac,scd->vsad/dot_general | solution.py:29
  70.3 0.6 dynamic_slice.71
  72.2 1.9 %fusion.32 = f32[4,1,256,256]{2,3,0,1:T(8,128)S(1)} fusion(f32[4,1,256,256]{2,3,0,1:T(8,128)S(1)} %get-tuple-element.245, bf16[4,3,256,256]{2,3,0,1:T(8,128)(2,1)S(1)} %get-tuple-element.258, s32[]{:T(128)S(6)} %select_n.28, pred[]{:T(512)S(6)} %compare.3, bf16[16,1,256,256]{3,2,1,0:T(8,128)(2,1)} %get-tuple-element.259, s32[]{:T(128)} %get-tuple-element.244, ...), kind=kOutput, calls=%fused_computation.1.clone.1 | convolution fusion | flops 269221888 | bytes 2884613 | tf_op jit(solution)/shard_map/while/body/eval_jaxpr/vsac,scd->vsad/dot_general | solution.py:29
  74.1 0.6 dynamic_slice.71
  76.0 1.9 %fusion.32 = f32[4,1,256,256]{2,3,0,1:T(8,128)S(1)} fusion(f32[4,1,256,256]{2,3,0,1:T(8,128)S(1)} %get-tuple-element.245, bf16[4,3,256,256]{2,3,0,1:T(8,128)(2,1)S(1)} %get-tuple-element.258, s32[]{:T(128)S(6)} %select_n.28, pred[]{:T(512)S(6)} %compare.3, bf16[16,1,256,256]{3,2,1,0:T(8,128)(2,1)} %get-tuple-element.259, s32[]{:T(128)} %get-tuple-element.244, ...), kind=kOutput, calls=%fused_computation.1.clone.1 | convolution fusion | flops 269221888 | bytes 2884613 | tf_op jit(solution)/shard_map/while/body/eval_jaxpr/vsac,scd->vsad/dot_general | solution.py:29
  77.9 0.6 dynamic_slice.71
  79.8 1.9 %fusion.32 = f32[4,1,256,256]{2,3,0,1:T(8,128)S(1)} fusion(f32[4,1,256,256]{2,3,0,1:T(8,128)S(1)} %get-tuple-element.245, bf16[4,3,256,256]{2,3,0,1:T(8,128)(2,1)S(1)} %get-tuple-element.258, s32[]{:T(128)S(6)} %select_n.28, pred[]{:T(512)S(6)} %compare.3, bf16[16,1,256,256]{3,2,1,0:T(8,128)(2,1)} %get-tuple-element.259, s32[]{:T(128)} %get-tuple-element.244, ...), kind=kOutput, calls=%fused_computation.1.clone.1 | convolution fusion | flops 269221888 | bytes 2884613 | tf_op jit(solution)/shard_map/while/body/eval_jaxpr/vsac,scd->vsad/dot_general | solution.py:29
  81.7 0.6 dynamic_slice.71
  83.6 1.9 %fusion.32 = f32[4,1,256,256]{2,3,0,1:T(8,128)S(1)} fusion(f32[4,1,256,256]{2,3,0,1:T(8,128)S(1)} %get-tuple-element.245, bf16[4,3,256,256]{2,3,0,1:T(8,128)(2,1)S(1)} %get-tuple-element.258, s32[]{:T(128)S(6)} %select_n.28, pred[]{:T(512)S(6)} %compare.3, bf16[16,1,256,256]{3,2,1,0:T(8,128)(2,1)} %get-tuple-element.259, s32[]{:T(128)} %get-tuple-element.244, ...), kind=kOutput, calls=%fused_computation.1.clone.1 | convolution fusion | flops 269221888 | bytes 2884613 | tf_op jit(solution)/shard_map/while/body/eval_jaxpr/vsac,scd->vsad/dot_general | solution.py:29
  85.5 0.6 dynamic_slice.71
  87.4 1.9 %fusion.32 = f32[4,1,256,256]{2,3,0,1:T(8,128)S(1)} fusion(f32[4,1,256,256]{2,3,0,1:T(8,128)S(1)} %get-tuple-element.245, bf16[4,3,256,256]{2,3,0,1:T(8,128)(2,1)S(1)} %get-tuple-element.258, s32[]{:T(128)S(6)} %select_n.28, pred[]{:T(512)S(6)} %compare.3, bf16[16,1,256,256]{3,2,1,0:T(8,128)(2,1)} %get-tuple-element.259, s32[]{:T(128)} %get-tuple-element.244, ...), kind=kOutput, calls=%fused_computation.1.clone.1 | convolution fusion | flops 269221888 | bytes 2884613 | tf_op jit(solution)/shard_map/while/body/eval_jaxpr/vsac,scd->vsad/dot_general | solution.py:29
  89.2 0.6 dynamic_slice.71
  91.1 1.9 %fusion.32 = f32[4,1,256,256]{2,3,0,1:T(8,128)S(1)} fusion(f32[4,1,256,256]{2,3,0,1:T(8,128)S(1)} %get-tuple-element.245, bf16[4,3,256,256]{2,3,0,1:T(8,128)(2,1)S(1)} %get-tuple-element.258, s32[]{:T(128)S(6)} %select_n.28, pred[]{:T(512)S(6)} %compare.3, bf16[16,1,256,256]{3,2,1,0:T(8,128)(2,1)} %get-tuple-element.259, s32[]{:T(128)} %get-tuple-element.244, ...), kind=kOutput, calls=%fused_computation.1.clone.1 | convolution fusion | flops 269221888 | bytes 2884613 | tf_op jit(solution)/shard_map/while/body/eval_jaxpr/vsac,scd->vsad/dot_general | solution.py:29
  93.0 0.6 dynamic_slice.71
  94.9 1.9 %fusion.32 = f32[4,1,256,256]{2,3,0,1:T(8,128)S(1)} fusion(f32[4,1,256,256]{2,3,0,1:T(8,128)S(1)} %get-tuple-element.245, bf16[4,3,256,256]{2,3,0,1:T(8,128)(2,1)S(1)} %get-tuple-element.258, s32[]{:T(128)S(6)} %select_n.28, pred[]{:T(512)S(6)} %compare.3, bf16[16,1,256,256]{3,2,1,0:T(8,128)(2,1)} %get-tuple-element.259, s32[]{:T(128)} %get-tuple-element.244, ...), kind=kOutput, calls=%fused_computation.1.clone.1 | convolution fusion | flops 269221888 | bytes 2884613 | tf_op jit(solution)/shard_map/while/body/eval_jaxpr/vsac,scd->vsad/dot_general | solution.py:29
  96.8 0.6 dynamic_slice.71
  98.7 1.9 %fusion.32 = f32[4,1,256,256]{2,3,0,1:T(8,128)S(1)} fusion(f32[4,1,256,256]{2,3,0,1:T(8,128)S(1)} %get-tuple-element.245, bf16[4,3,256,256]{2,3,0,1:T(8,128)(2,1)S(1)} %get-tuple-element.258, s32[]{:T(128)S(6)} %select_n.28, pred[]{:T(512)S(6)} %compare.3, bf16[16,1,256,256]{3,2,1,0:T(8,128)(2,1)} %get-tuple-element.259, s32[]{:T(128)} %get-tuple-element.244, ...), kind=kOutput, calls=%fused_computation.1.clone.1 | convolution fusion | flops 269221888 | bytes 2884613 | tf_op jit(solution)/shard_map/while/body/eval_jaxpr/vsac,scd->vsad/dot_general | solution.py:29
  100.6 0.6 dynamic_slice.71
  102.5 1.9 %fusion.32 = f32[4,1,256,256]{2,3,0,1:T(8,128)S(1)} fusion(f32[4,1,256,256]{2,3,0,1:T(8,128)S(1)} %get-tuple-element.245, bf16[4,3,256,256]{2,3,0,1:T(8,128)(2,1)S(1)} %get-tuple-element.258, s32[]{:T(128)S(6)} %select_n.28, pred[]{:T(512)S(6)} %compare.3, bf16[16,1,256,256]{3,2,1,0:T(8,128)(2,1)} %get-tuple-element.259, s32[]{:T(128)} %get-tuple-element.244, ...), kind=kOutput, calls=%fused_computation.1.clone.1 | convolution fusion | flops 269221888 | bytes 2884613 | tf_op jit(solution)/shard_map/while/body/eval_jaxpr/vsac,scd->vsad/dot_general | solution.py:29
  104.4 0.6 dynamic_slice.71
  106.3 1.9 %fusion.32 = f32[4,1,256,256]{2,3,0,1:T(8,128)S(1)} fusion(f32[4,1,256,256]{2,3,0,1:T(8,128)S(1)} %get-tuple-element.245, bf16[4,3,256,256]{2,3,0,1:T(8,128)(2,1)S(1)} %get-tuple-element.258, s32[]{:T(128)S(6)} %select_n.28, pred[]{:T(512)S(6)} %compare.3, bf16[16,1,256,256]{3,2,1,0:T(8,128)(2,1)} %get-tuple-element.259, s32[]{:T(128)} %get-tuple-element.244, ...), kind=kOutput, calls=%fused_computation.1.clone.1 | convolution fusion | flops 269221888 | bytes 2884613 | tf_op jit(solution)/shard_map/while/body/eval_jaxpr/vsac,scd->vsad/dot_general | solution.py:29
  108.1 0.6 dynamic_slice.71
  110.0 1.9 %fusion.32 = f32[4,1,256,256]{2,3,0,1:T(8,128)S(1)} fusion(f32[4,1,256,256]{2,3,0,1:T(8,128)S(1)} %get-tuple-element.245, bf16[4,3,256,256]{2,3,0,1:T(8,128)(2,1)S(1)} %get-tuple-element.258, s32[]{:T(128)S(6)} %select_n.28, pred[]{:T(512)S(6)} %compare.3, bf16[16,1,256,256]{3,2,1,0:T(8,128)(2,1)} %get-tuple-element.259, s32[]{:T(128)} %get-tuple-element.244, ...), kind=kOutput, calls=%fused_computation.1.clone.1 | convolution fusion | flops 269221888 | bytes 2884613 | tf_op jit(solution)/shard_map/while/body/eval_jaxpr/vsac,scd->vsad/dot_general | solution.py:29
  111.9 0.6 dynamic_slice.71
  113.8 1.9 %fusion.32 = f32[4,1,256,256]{2,3,0,1:T(8,128)S(1)} fusion(f32[4,1,256,256]{2,3,0,1:T(8,128)S(1)} %get-tuple-element.245, bf16[4,3,256,256]{2,3,0,1:T(8,128)(2,1)S(1)} %get-tuple-element.258, s32[]{:T(128)S(6)} %select_n.28, pred[]{:T(512)S(6)} %compare.3, bf16[16,1,256,256]{3,2,1,0:T(8,128)(2,1)} %get-tuple-element.259, s32[]{:T(128)} %get-tuple-element.244, ...), kind=kOutput, calls=%fused_computation.1.clone.1 | convolution fusion | flops 269221888 | bytes 2884613 | tf_op jit(solution)/shard_map/while/body/eval_jaxpr/vsac,scd->vsad/dot_general | solution.py:29
  115.7 0.6 dynamic_slice.71
  117.6 1.9 %fusion.32 = f32[4,1,256,256]{2,3,0,1:T(8,128)S(1)} fusion(f32[4,1,256,256]{2,3,0,1:T(8,128)S(1)} %get-tuple-element.245, bf16[4,3,256,256]{2,3,0,1:T(8,128)(2,1)S(1)} %get-tuple-element.258, s32[]{:T(128)S(6)} %select_n.28, pred[]{:T(512)S(6)} %compare.3, bf16[16,1,256,256]{3,2,1,0:T(8,128)(2,1)} %get-tuple-element.259, s32[]{:T(128)} %get-tuple-element.244, ...), kind=kOutput, calls=%fused_computation.1.clone.1 | convolution fusion | flops 269221888 | bytes 2884613 | tf_op jit(solution)/shard_map/while/body/eval_jaxpr/vsac,scd->vsad/dot_general | solution.py:29
  119.7 3.3 %fusion.21 = f32[16,4]{1,0:T(8,128)S(1)} fusion(bf16[16,256,256]{2,1,0:T(8,128)(2,1)} %bitcast.56, bf16[4,256,256]{2,1,0:T(8,128)(2,1)S(1)} %bitcast.54), kind=kOutput, calls=%fused_computation.17 | convolution fusion | flops 8388608 | bytes 2621696 | tf_op jit(solution)/shard_map/isab,jsab->ij/dot_general | solution.py:50
  123.0 0.2 dynamic_update_slice.3
  123.2 39.4 %psum.15 = f32[16,16]{1,0:T(8,128)S(1)} all-reduce(f32[16,16]{1,0:T(8,128)S(1)} %dynamic_update_slice.3), channel_id=1, replica_groups=mesh['sector'=8,'mpo'=4] {'sector','mpo'}, use_global_device_ids=true, to_apply=%region_3.4 | all-reduce | flops 256 | bytes 2048 | tf_op jit(solution)/shard_map/psum | solution.py:56
  162.6 0.6 broadcast_multiply_fusion
  (14 shorter events, 0.5 us)
Async XLA Ops:
  7.2 45.7 %all-gather.3.cloned.1.call-start = ((), (), s32[]{:S(2)}) async-start(), calls=%async_computation | async-start | bytes 2621440 | tf_op jit(solution)/shard_map/all_gather | solution.py:40
  7.9 51.1 %all-gather.5.cloned.1.call-start = ((), (), s32[]{:S(2)}) async-start(), calls=%async_computation.1 | async-start | bytes 2621440 | tf_op jit(solution)/shard_map/all_gather | solution.py:39
  9.9 40.7 %collective-permute-start = (bf16[4,1,256,256]{2,3,0,1:T(8,128)(2,1)S(1)}, bf16[4,1,256,256]{2,3,0,1:T(8,128)(2,1)S(1)}, u32[]{:S(2)}, u32[]{:S(2)}) collective-permute-start(bf16[4,1,256,256]{2,3,0,1:T(8,128)(2,1)S(1)} %copy.29), channel_id=1, source_target_pairs={{0,4},{4,8},{8,12},{12,16},{16,20},{20,24},{24,28},{1,5},{5,9},{9,... | collective-permute-start | bytes 1572872 | tf_op jit(solution)/shard_map/ppermute | solution.py:15
  14.9 36.5 %collective-permute-start.1 = (bf16[4,1,256,256]{2,3,0,1:T(8,128)(2,1)S(1)}, bf16[4,1,256,256]{2,3,0,1:T(8,128)(2,1)}, u32[]{:S(2)}, u32[]{:S(2)}) collective-permute-start(bf16[4,1,256,256]{2,3,0,1:T(8,128)(2,1)S(1)} %copy.29), channel_id=1, source_target_pairs={{4,0},{8,4},{12,8},{16,12},{20,16},{24,20},{28,24},{5,1},{9,5},{13... | collective-permute-start | bytes 1572872 | tf_op jit(solution)/shard_map/ppermute | solution.py:17
  21.1 38.0 %copy-start.2 = (s32[16]{0:T(128)S(1)}, s32[16]{0:T(128)}, u32[]{:S(2)}) copy-start(s32[16]{0:T(128)} %param.9) | copy-start | bytes 196
  50.6 0.8 copy-start.1
  119.7 3.3 %copy-start = (bf16[4,1,256,256]{3,2,1,0:T(8,128)(2,1)}, bf16[4,1,256,256]{3,2,1,0:T(8,128)(2,1)S(1)}, u32[]{:S(2)}) copy-start(bf16[4,1,256,256]{3,2,1,0:T(8,128)(2,1)S(1)} %copy.19) | copy-start | bytes 1572868
Sparse Core Ops, SparseCore 0:
  9.5 25.2 all-gather.2
  36.4 22.5 all-gather.4
where the time goes:
time: 171 us; the launch traced here: 170 us
  blocking collectives  68.3 us (40%)
  matrix products  38 us (22%)
  loops' own time  21.2 us (12%)
  between operations  14.1 us (8%)
  local copies, waits for them, and re-layouts  11.9 us (7%)
  waiting for transfers between devices  7.58 us (4%)
  starting transfers between devices  6.3 us (4%)
  other arithmetic  2.58 us (2%)
    psum x1, blocking collectives, body(): ham_small = lax.psum(ham_part, ('sector', 'mpo'))  39.4 us
    dot_general x16, matrix products, bond_term(): jnp.einsum('vsac,scd->vsad', left, renv, preferred_element_type=jnp.float32)  29.9 us
    psum x1, blocking collectives, body(): intersection = lax.psum(full_intersection, 'sector')  29 us
    another operation x1, loops' own time, body(): summed = lax.fori_loop(0, lpiece.shape[0], step, empty)  21.2 us
    dynamic_slice x16, local copies, waits for them, and re-layouts, step(): shift = lax.dynamic_index_in_dim(bond_shift, index, 0, keepdims=False)  9.38 us
    all_gather x1, waiting for transfers between devices, body(): lpiece = lax.all_gather(left_env, 'mpo', axis=0, tiled=True)  6.17 us
    ppermute x1, starting transfers between devices, with_halo(): lax.ppermute(tail, axis, [(i, (i + 1) % count) for i in range(ends)])  4.93 us
    dot_general x1, matrix products, body(): jnp.einsum('isab,jsab->ij', vectors, vectors, preferred_element_type=jnp....  4.86 us
  transfers between devices with their start and end apart: 4, of which 1 were waited for; matrix products, arithmetic and copies ran while one was open for 5% of the time, Pallas kernels for 0%

commit v1 on v0

--- a/solution.py
+++ b/solution.py
@@ -52,7 +52,8 @@
     full_intersection = jnp.einsum(
         "isab,jsab->ij", vectors, vectors, preferred_element_type=jnp.float32
     )
-    intersection = lax.psum(full_intersection, "sector")
+    terms = lax.all_gather(full_intersection, "sector", axis=0, tiled=False)
+    intersection = terms.sum(axis=0)
     ham_small = lax.psum(ham_part, ("sector", "mpo"))
     return (sigma, intersection * scale, ham_small * scale)
 

time: 171 us -> 177 us (1.035)
  blocking collectives: 68.3 us -> 79.2 us
  waiting for transfers between devices: 7.58 us -> 1.42 us
    all_gather x0 -> x1, blocking collectives: none -> 42.3 us  [body(): terms = lax.all_gather(full_intersection, 'sector', axis=0, tiled=False)]
    psum x1 -> x0, blocking collectives: 29 us -> none  [body(): intersection = lax.psum(full_intersection, 'sector')]
    all_gather x1, waiting for transfers between devices: 6.17 us -> 0.02 us  [body(): lpiece = lax.all_gather(left_env, 'mpo', axis=0, tiled=True)]
    psum x1, blocking collectives: 39.4 us -> 36.9 us  [body(): ham_small = lax.psum(ham_part, ('sector', 'mpo'))]
  transfers between devices with their start and end apart: 4 -> 4, of which waited for: 1 -> 0; matrix products, arithmetic and copies ran while one was open for 5% -> 5% of each run, Pallas kernels for 0% -> 0%
where the time goes in v1:
time: 177 us; the launch traced here: 175 us
  blocking collectives  79.2 us (45%)
  matrix products  38.3 us (22%)
  loops' own time  21.2 us (12%)
  between operations  14.1 us (8%)
  local copies, waits for them, and re-layouts  11.9 us (7%)
  starting transfers between devices  6.3 us (4%)
  other arithmetic  2.59 us (1%)
    all_gather x1, blocking collectives, body(): terms = lax.all_gather(full_intersection, 'sector', axis=0, tiled=False)  42.3 us
    psum x1, blocking collectives, body(): ham_small = lax.psum(ham_part, ('sector', 'mpo'))  36.9 us
    dot_general x16, matrix products, bond_term(): jnp.einsum('vsac,scd->vsad', left, renv, preferred_element_type=jnp.float32)  29.9 us
    another operation x1, loops' own time, body(): summed = lax.fori_loop(0, lpiece.shape[0], step, empty)  21.2 us
    dynamic_slice x16, local copies, waits for them, and re-layouts, step(): shift = lax.dynamic_index_in_dim(bond_shift, index, 0, keepdims=False)  9.38 us
    ppermute x1, starting transfers between devices, with_halo(): lax.ppermute(tail, axis, [(i, (i + 1) % count) for i in range(ends)])  4.93 us
    dot_general x1, matrix products, body(): jnp.einsum('isab,jsab->ij', vectors, vectors, preferred_element_type=jnp....  4.86 us
    dot_general x1, matrix products, body(): jnp.einsum('isab,jsab->ij', vectors, sigma, preferred_element_type=jnp.fl...  3.64 us
  transfers between devices with their start and end apart: 4, of which 0 were waited for; matrix products, arithmetic and copies ran while one was open for 5% of the time, Pallas kernels for 0%

profile of v1, /device:TPU:0, one launch (start us, length us, event | category | flops | bytes accessed | tf_op | source)
XLA Modules:
  0.0 175.2 jit_solution(11752005464448803224)
XLA Ops:
  7.2 0.7 all-gather.4.cloned.1.call-update
  7.9 0.7 all-gather.6.cloned.1.call-update
  8.7 1.1 constant_dynamic-slice_fusion
  9.7 0.2 copy.27
  9.9 4.9 %collective-permute-start = (bf16[4,1,256,256]{2,3,0,1:T(8,128)(2,1)S(1)}, bf16[4,1,256,256]{2,3,0,1:T(8,128)(2,1)S(1)}, u32[]{:S(2)}, u32[]{:S(2)}) collective-permute-start(bf16[4,1,256,256]{2,3,0,1:T(8,128)(2,1)S(1)} %copy.27), channel_id=1, source_target_pairs={{0,4},{4,8},{8,12},{12,16},{16,20},{20,24},{24,28},{1,5},{5,9},{9,... | collective-permute-start | bytes 1572872 | tf_op jit(solution)/shard_map/ppermute | solution.py:15
  14.9 1.3 collective-permute-start.1
  16.2 4.9 %fusion.18 = f32[16,16]{1,0:T(8,128)S(1)} fusion(bf16[16,256,256]{2,1,0:T(8,128)(2,1)} %bitcast.57), kind=kOutput, calls=%fused_computation.16 | convolution fusion | flops 33554432 | bytes 2098176 | tf_op jit(solution)/shard_map/isab,jsab->ij/dot_general | solution.py:52
  21.1 42.3 %all-gather = f32[128,16]{1,0:T(8,128)S(1)} all-gather(f32[16,16]{1,0:T(8,128)S(1)} %fusion.18), channel_id=2, replica_groups=mesh['sector'=8,'mpo'=4] {'sector'}, dimensions={0}, use_global_device_ids=true | all-gather | bytes 9216 | tf_op jit(solution)/shard_map/all_gather | solution.py:55
  63.4 0.6 broadcast_multiply_fusion.1
  64.0 0.8 copy-done.1
  64.8 1.4 pad_maximum_fusion
  66.2 60.5 %while.16 = (s32[]{:T(128)}, f32[4,1,256,256]{2,3,0,1:T(8,128)S(1)}, bf16[16,1,256,256]{3,2,1,0:T(8,128)(2,1)}, s32[16]{0:T(128)S(1)}, bf16[4,3,256,256]{2,3,0,1...) while((s32[]{:T(128)}, ...), condition=%wide.region_1.2_spmd.clone, body=%wide.region_0.1_spmd.clone.sunk | while | flops 269221888 | bytes 2884781 | solution.py:46
  66.2 0.6 dynamic_slice.71
  68.1 1.9 %fusion.32 = f32[4,1,256,256]{2,3,0,1:T(8,128)S(1)} fusion(f32[4,1,256,256]{2,3,0,1:T(8,128)S(1)} %get-tuple-element.245, bf16[4,3,256,256]{2,3,0,1:T(8,128)(2,1)S(1)} %get-tuple-element.258, s32[]{:T(128)S(6)} %select_n.28, pred[]{:T(512)S(6)} %compare.3, bf16[16,1,256,256]{3,2,1,0:T(8,128)(2,1)} %get-tuple-element.259, s32[]{:T(128)} %get-tuple-element.244, ...), kind=kOutput, calls=%fused_computation.1.clone.1 | convolution fusion | flops 269221888 | bytes 2884613 | tf_op jit(solution)/shard_map/while/body/eval_jaxpr/vsac,scd->vsad/dot_general | solution.py:29
  70.0 0.6 dynamic_slice.71
  71.9 1.9 %fusion.32 = f32[4,1,256,256]{2,3,0,1:T(8,128)S(1)} fusion(f32[4,1,256,256]{2,3,0,1:T(8,128)S(1)} %get-tuple-element.245, bf16[4,3,256,256]{2,3,0,1:T(8,128)(2,1)S(1)} %get-tuple-element.258, s32[]{:T(128)S(6)} %select_n.28, pred[]{:T(512)S(6)} %compare.3, bf16[16,1,256,256]{3,2,1,0:T(8,128)(2,1)} %get-tuple-element.259, s32[]{:T(128)} %get-tuple-element.244, ...), kind=kOutput, calls=%fused_computation.1.clone.1 | convolution fusion | flops 269221888 | bytes 2884613 | tf_op jit(solution)/shard_map/while/body/eval_jaxpr/vsac,scd->vsad/dot_general | solution.py:29
  73.8 0.6 dynamic_slice.71
  75.7 1.9 %fusion.32 = f32[4,1,256,256]{2,3,0,1:T(8,128)S(1)} fusion(f32[4,1,256,256]{2,3,0,1:T(8,128)S(1)} %get-tuple-element.245, bf16[4,3,256,256]{2,3,0,1:T(8,128)(2,1)S(1)} %get-tuple-element.258, s32[]{:T(128)S(6)} %select_n.28, pred[]{:T(512)S(6)} %compare.3, bf16[16,1,256,256]{3,2,1,0:T(8,128)(2,1)} %get-tuple-element.259, s32[]{:T(128)} %get-tuple-element.244, ...), kind=kOutput, calls=%fused_computation.1.clone.1 | convolution fusion | flops 269221888 | bytes 2884613 | tf_op jit(solution)/shard_map/while/body/eval_jaxpr/vsac,scd->vsad/dot_general | solution.py:29
  77.6 0.6 dynamic_slice.71
  79.5 1.9 %fusion.32 = f32[4,1,256,256]{2,3,0,1:T(8,128)S(1)} fusion(f32[4,1,256,256]{2,3,0,1:T(8,128)S(1)} %get-tuple-element.245, bf16[4,3,256,256]{2,3,0,1:T(8,128)(2,1)S(1)} %get-tuple-element.258, s32[]{:T(128)S(6)} %select_n.28, pred[]{:T(512)S(6)} %compare.3, bf16[16,1,256,256]{3,2,1,0:T(8,128)(2,1)} %get-tuple-element.259, s32[]{:T(128)} %get-tuple-element.244, ...), kind=kOutput, calls=%fused_computation.1.clone.1 | convolution fusion | flops 269221888 | bytes 2884613 | tf_op jit(solution)/shard_map/while/body/eval_jaxpr/vsac,scd->vsad/dot_general | solution.py:29
  81.4 0.6 dynamic_slice.71
  83.2 1.9 %fusion.32 = f32[4,1,256,256]{2,3,0,1:T(8,128)S(1)} fusion(f32[4,1,256,256]{2,3,0,1:T(8,128)S(1)} %get-tuple-element.245, bf16[4,3,256,256]{2,3,0,1:T(8,128)(2,1)S(1)} %get-tuple-element.258, s32[]{:T(128)S(6)} %select_n.28, pred[]{:T(512)S(6)} %compare.3, bf16[16,1,256,256]{3,2,1,0:T(8,128)(2,1)} %get-tuple-element.259, s32[]{:T(128)} %get-tuple-element.244, ...), kind=kOutput, calls=%fused_computation.1.clone.1 | convolution fusion | flops 269221888 | bytes 2884613 | tf_op jit(solution)/shard_map/while/body/eval_jaxpr/vsac,scd->vsad/dot_general | solution.py:29
  85.1 0.6 dynamic_slice.71
  87.0 1.9 %fusion.32 = f32[4,1,256,256]{2,3,0,1:T(8,128)S(1)} fusion(f32[4,1,256,256]{2,3,0,1:T(8,128)S(1)} %get-tuple-element.245, bf16[4,3,256,256]{2,3,0,1:T(8,128)(2,1)S(1)} %get-tuple-element.258, s32[]{:T(128)S(6)} %select_n.28, pred[]{:T(512)S(6)} %compare.3, bf16[16,1,256,256]{3,2,1,0:T(8,128)(2,1)} %get-tuple-element.259, s32[]{:T(128)} %get-tuple-element.244, ...), kind=kOutput, calls=%fused_computation.1.clone.1 | convolution fusion | flops 269221888 | bytes 2884613 | tf_op jit(solution)/shard_map/while/body/eval_jaxpr/vsac,scd->vsad/dot_general | solution.py:29
  88.9 0.6 dynamic_slice.71
  90.8 1.9 %fusion.32 = f32[4,1,256,256]{2,3,0,1:T(8,128)S(1)} fusion(f32[4,1,256,256]{2,3,0,1:T(8,128)S(1)} %get-tuple-element.245, bf16[4,3,256,256]{2,3,0,1:T(8,128)(2,1)S(1)} %get-tuple-element.258, s32[]{:T(128)S(6)} %select_n.28, pred[]{:T(512)S(6)} %compare.3, bf16[16,1,256,256]{3,2,1,0:T(8,128)(2,1)} %get-tuple-element.259, s32[]{:T(128)} %get-tuple-element.244, ...), kind=kOutput, calls=%fused_computation.1.clone.1 | convolution fusion | flops 269221888 | bytes 2884613 | tf_op jit(solution)/shard_map/while/body/eval_jaxpr/vsac,scd->vsad/dot_general | solution.py:29
  92.7 0.6 dynamic_slice.71
  94.6 1.9 %fusion.32 = f32[4,1,256,256]{2,3,0,1:T(8,128)S(1)} fusion(f32[4,1,256,256]{2,3,0,1:T(8,128)S(1)} %get-tuple-element.245, bf16[4,3,256,256]{2,3,0,1:T(8,128)(2,1)S(1)} %get-tuple-element.258, s32[]{:T(128)S(6)} %select_n.28, pred[]{:T(512)S(6)} %compare.3, bf16[16,1,256,256]{3,2,1,0:T(8,128)(2,1)} %get-tuple-element.259, s32[]{:T(128)} %get-tuple-element.244, ...), kind=kOutput, calls=%fused_computation.1.clone.1 | convolution fusion | flops 269221888 | bytes 2884613 | tf_op jit(solution)/shard_map/while/body/eval_jaxpr/vsac,scd->vsad/dot_general | solution.py:29
  96.5 0.6 dynamic_slice.71
  98.4 1.9 %fusion.32 = f32[4,1,256,256]{2,3,0,1:T(8,128)S(1)} fusion(f32[4,1,256,256]{2,3,0,1:T(8,128)S(1)} %get-tuple-element.245, bf16[4,3,256,256]{2,3,0,1:T(8,128)(2,1)S(1)} %get-tuple-element.258, s32[]{:T(128)S(6)} %select_n.28, pred[]{:T(512)S(6)} %compare.3, bf16[16,1,256,256]{3,2,1,0:T(8,128)(2,1)} %get-tuple-element.259, s32[]{:T(128)} %get-tuple-element.244, ...), kind=kOutput, calls=%fused_computation.1.clone.1 | convolution fusion | flops 269221888 | bytes 2884613 | tf_op jit(solution)/shard_map/while/body/eval_jaxpr/vsac,scd->vsad/dot_general | solution.py:29
  100.3 0.6 dynamic_slice.71
  102.1 1.9 %fusion.32 = f32[4,1,256,256]{2,3,0,1:T(8,128)S(1)} fusion(f32[4,1,256,256]{2,3,0,1:T(8,128)S(1)} %get-tuple-element.245, bf16[4,3,256,256]{2,3,0,1:T(8,128)(2,1)S(1)} %get-tuple-element.258, s32[]{:T(128)S(6)} %select_n.28, pred[]{:T(512)S(6)} %compare.3, bf16[16,1,256,256]{3,2,1,0:T(8,128)(2,1)} %get-tuple-element.259, s32[]{:T(128)} %get-tuple-element.244, ...), kind=kOutput, calls=%fused_computation.1.clone.1 | convolution fusion | flops 269221888 | bytes 2884613 | tf_op jit(solution)/shard_map/while/body/eval_jaxpr/vsac,scd->vsad/dot_general | solution.py:29
  104.0 0.6 dynamic_slice.71
  105.9 1.9 %fusion.32 = f32[4,1,256,256]{2,3,0,1:T(8,128)S(1)} fusion(f32[4,1,256,256]{2,3,0,1:T(8,128)S(1)} %get-tuple-element.245, bf16[4,3,256,256]{2,3,0,1:T(8,128)(2,1)S(1)} %get-tuple-element.258, s32[]{:T(128)S(6)} %select_n.28, pred[]{:T(512)S(6)} %compare.3, bf16[16,1,256,256]{3,2,1,0:T(8,128)(2,1)} %get-tuple-element.259, s32[]{:T(128)} %get-tuple-element.244, ...), kind=kOutput, calls=%fused_computation.1.clone.1 | convolution fusion | flops 269221888 | bytes 2884613 | tf_op jit(solution)/shard_map/while/body/eval_jaxpr/vsac,scd->vsad/dot_general | solution.py:29
  107.8 0.6 dynamic_slice.71
  109.7 1.9 %fusion.32 = f32[4,1,256,256]{2,3,0,1:T(8,128)S(1)} fusion(f32[4,1,256,256]{2,3,0,1:T(8,128)S(1)} %get-tuple-element.245, bf16[4,3,256,256]{2,3,0,1:T(8,128)(2,1)S(1)} %get-tuple-element.258, s32[]{:T(128)S(6)} %select_n.28, pred[]{:T(512)S(6)} %compare.3, bf16[16,1,256,256]{3,2,1,0:T(8,128)(2,1)} %get-tuple-element.259, s32[]{:T(128)} %get-tuple-element.244, ...), kind=kOutput, calls=%fused_computation.1.clone.1 | convolution fusion | flops 269221888 | bytes 2884613 | tf_op jit(solution)/shard_map/while/body/eval_jaxpr/vsac,scd->vsad/dot_general | solution.py:29
  111.6 0.6 dynamic_slice.71
  113.5 1.9 %fusion.32 = f32[4,1,256,256]{2,3,0,1:T(8,128)S(1)} fusion(f32[4,1,256,256]{2,3,0,1:T(8,128)S(1)} %get-tuple-element.245, bf16[4,3,256,256]{2,3,0,1:T(8,128)(2,1)S(1)} %get-tuple-element.258, s32[]{:T(128)S(6)} %select_n.28, pred[]{:T(512)S(6)} %compare.3, bf16[16,1,256,256]{3,2,1,0:T(8,128)(2,1)} %get-tuple-element.259, s32[]{:T(128)} %get-tuple-element.244, ...), kind=kOutput, calls=%fused_computation.1.clone.1 | convolution fusion | flops 269221888 | bytes 2884613 | tf_op jit(solution)/shard_map/while/body/eval_jaxpr/vsac,scd->vsad/dot_general | solution.py:29
  115.4 0.6 dynamic_slice.71
  117.3 1.9 %fusion.32 = f32[4,1,256,256]{2,3,0,1:T(8,128)S(1)} fusion(f32[4,1,256,256]{2,3,0,1:T(8,128)S(1)} %get-tuple-element.245, bf16[4,3,256,256]{2,3,0,1:T(8,128)(2,1)S(1)} %get-tuple-element.258, s32[]{:T(128)S(6)} %select_n.28, pred[]{:T(512)S(6)} %compare.3, bf16[16,1,256,256]{3,2,1,0:T(8,128)(2,1)} %get-tuple-element.259, s32[]{:T(128)} %get-tuple-element.244, ...), kind=kOutput, calls=%fused_computation.1.clone.1 | convolution fusion | flops 269221888 | bytes 2884613 | tf_op jit(solution)/shard_map/while/body/eval_jaxpr/vsac,scd->vsad/dot_general | solution.py:29
  119.2 0.6 dynamic_slice.71
  121.0 1.9 %fusion.32 = f32[4,1,256,256]{2,3,0,1:T(8,128)S(1)} fusion(f32[4,1,256,256]{2,3,0,1:T(8,128)S(1)} %get-tuple-element.245, bf16[4,3,256,256]{2,3,0,1:T(8,128)(2,1)S(1)} %get-tuple-element.258, s32[]{:T(128)S(6)} %select_n.28, pred[]{:T(512)S(6)} %compare.3, bf16[16,1,256,256]{3,2,1,0:T(8,128)(2,1)} %get-tuple-element.259, s32[]{:T(128)} %get-tuple-element.244, ...), kind=kOutput, calls=%fused_computation.1.clone.1 | convolution fusion | flops 269221888 | bytes 2884613 | tf_op jit(solution)/shard_map/while/body/eval_jaxpr/vsac,scd->vsad/dot_general | solution.py:29
  122.9 0.6 dynamic_slice.71
  124.8 1.9 %fusion.32 = f32[4,1,256,256]{2,3,0,1:T(8,128)S(1)} fusion(f32[4,1,256,256]{2,3,0,1:T(8,128)S(1)} %get-tuple-element.245, bf16[4,3,256,256]{2,3,0,1:T(8,128)(2,1)S(1)} %get-tuple-element.258, s32[]{:T(128)S(6)} %select_n.28, pred[]{:T(512)S(6)} %compare.3, bf16[16,1,256,256]{3,2,1,0:T(8,128)(2,1)} %get-tuple-element.259, s32[]{:T(128)} %get-tuple-element.244, ...), kind=kOutput, calls=%fused_computation.1.clone.1 | convolution fusion | flops 269221888 | bytes 2884613 | tf_op jit(solution)/shard_map/while/body/eval_jaxpr/vsac,scd->vsad/dot_general | solution.py:29
  126.7 0.2 copy.19
  126.9 3.6 %fusion.21 = f32[16,4]{0,1:T(4,128)S(1)} fusion(bf16[16,256,256]{2,1,0:T(8,128)(2,1)} %bitcast.58, bf16[4,256,256]{2,1,0:T(8,128)(2,1)S(1)} %bitcast.55), kind=kOutput, calls=%fused_computation.17 | convolution fusion | flops 8388608 | bytes 2621696 | tf_op jit(solution)/shard_map/isab,jsab->ij/dot_general | solution.py:50
  130.8 36.9 %psum.7 = f32[16,16]{1,0:T(8,128)S(1)} all-reduce(f32[16,16]{1,0:T(8,128)S(1)} %dynamic_update_slice.3), channel_id=1, replica_groups=mesh['sector'=8,'mpo'=4] {'sector','mpo'}, use_global_device_ids=true, to_apply=%region_3.4 | all-reduce | flops 256 | bytes 2048 | tf_op jit(solution)/shard_map/psum | solution.py:57
  167.7 0.6 broadcast_multiply_fusion
  (16 shorter events, 0.4 us)
Async XLA Ops:
  7.2 59.0 %all-gather.4.cloned.1.call-start = ((), (), s32[]{:S(2)}) async-start(), calls=%async_computation | async-start | bytes 2621440 | tf_op jit(solution)/shard_map/all_gather | solution.py:40
  7.9 58.3 %all-gather.6.cloned.1.call-start = ((), (), s32[]{:S(2)}) async-start(), calls=%async_computation.1 | async-start | bytes 2621440 | tf_op jit(solution)/shard_map/all_gather | solution.py:39
  9.9 54.0 %collective-permute-start = (bf16[4,1,256,256]{2,3,0,1:T(8,128)(2,1)S(1)}, bf16[4,1,256,256]{2,3,0,1:T(8,128)(2,1)S(1)}, u32[]{:S(2)}, u32[]{:S(2)}) collective-permute-start(bf16[4,1,256,256]{2,3,0,1:T(8,128)(2,1)S(1)} %copy.27), channel_id=1, source_target_pairs={{0,4},{4,8},{8,12},{12,16},{16,20},{20,24},{24,28},{1,5},{5,9},{9,... | collective-permute-start | bytes 1572872 | tf_op jit(solution)/shard_map/ppermute | solution.py:15
  14.9 49.9 %collective-permute-start.1 = (bf16[4,1,256,256]{2,3,0,1:T(8,128)(2,1)S(1)}, bf16[4,1,256,256]{2,3,0,1:T(8,128)(2,1)}, u32[]{:S(2)}, u32[]{:S(2)}) collective-permute-start(bf16[4,1,256,256]{2,3,0,1:T(8,128)(2,1)S(1)} %copy.27), channel_id=1, source_target_pairs={{4,0},{8,4},{12,8},{16,12},{20,16},{24,20},{28,24},{5,1},{9,5},{13... | collective-permute-start | bytes 1572872 | tf_op jit(solution)/shard_map/ppermute | solution.py:17
  21.1 45.2 %copy-start.2 = (s32[16]{0:T(128)S(1)}, s32[16]{0:T(128)}, u32[]{:S(2)}) copy-start(s32[16]{0:T(128)} %param.9) | copy-start | bytes 196
  64.0 0.8 copy-start.1
  126.9 41.4 %copy-start = (bf16[4,1,256,256]{3,2,1,0:T(8,128)(2,1)}, bf16[4,1,256,256]{3,2,1,0:T(8,128)(2,1)S(1)}, u32[]{:S(2)}) copy-start(bf16[4,1,256,256]{3,2,1,0:T(8,128)(2,1)S(1)} %copy.19) | copy-start | bytes 1572868
Sparse Core Ops, SparseCore 0:
  9.5 25.2 all-gather.3
  36.4 22.5 all-gather.5
